TPU v7x, 128 devices: a whole 4x4x4 slice. The times are simulated.
128 devices in a mesh: gene: 8 (over y, x_lo), bin: 16 (over z, x_hi, core).
Axes of the slice: x: 4 (x_hi: 2, x_lo: 2; x = x_hi * 2 + x_lo), y: 4, z: 4, core: 2. Of those that a mesh axis runs over, the one named last changes fastest.
Arguments:
- counts: bfloat16 [49152, 18432], P('bin', 'gene'), may hold values from 2 to 80
- factors: float32 [49152, 256], P('bin'), may hold values from 0.01 to 1
- loadings: float32 [256, 18432], P(None, 'gene'), may hold values from 0.01 to 1
- position: int32 [49152], P('bin'), may hold values from 0 to 49151, as said below
- edge_codes: int32 [192, 256], P('bin'), may hold values from 1 to 15
Outputs:
- factors_new: float32 [49152, 256], P('bin')
- loadings_new: float32 [256, 18432], P(None, 'gene')
Inputs may be any that keep to these rules, and one draw needn't show every extreme that they name: Each grid position is named by exactly one barcode. The barcodes of one index s of bin (rows s * 3072 on) fall in 16 aligned groups of 192; group t holds positions in grid rows t * 12 to (t + 1) * 12 - 1, 192 from every such index.
All inputs are finite; a program needn't handle non-finite values.
Results may differ from a plain program's by a relative error of at most 0.0003.
Values sent between devices are 32-bit elements; how exact they have to be, the bound alone decides.
A program may use at most 128 MiB of HBM per device.

v0:
```python
import jax
import jax.numpy as jnp
from jax import lax
from jax.sharding import PartitionSpec as P

K = 256
G = 18432


def passed_along(block, axis, distance):
    devices = range(lax.axis_size(axis))
    route = [(i - distance, i) for i in devices if i - distance in devices]
    return lax.ppermute(block, axis, route)


def neighbour_sum(values, from_above, from_below):
    upper = jnp.concatenate([from_above[None], values[:-1]], 0)
    lower = jnp.concatenate([values[1:], from_below[None]], 0)
    beside = jnp.pad(values[:, 1:], ((0, 0), (0, 1), (0, 0))) + jnp.pad(
        values[:, :-1], ((0, 0), (1, 0), (0, 0))
    )
    return beside + 0.5 * (lower + upper)


def neighbour_first(values, from_above, from_below):
    upper = jnp.concatenate([from_above[:, None], values[:, :-1]], 1)
    lower = jnp.concatenate([values[:, 1:], from_below[:, None]], 1)
    beside = jnp.pad(values[:, :, 1:], ((0, 0), (0, 0), (0, 1))) + jnp.pad(
        values[:, :, :-1], ((0, 0), (0, 0), (1, 0))
    )
    return beside + 0.5 * (lower + upper)


def split_three(values):
    high = lax.reduce_precision(values, exponent_bits=8, mantissa_bits=7)
    rest = values - high
    mid = lax.reduce_precision(rest, exponent_bits=8, mantissa_bits=7)
    low = rest - mid
    return jnp.concatenate([high, mid, low], 1).astype(jnp.bfloat16)


def join_three(parts, width):
    return parts[:, :width] + parts[:, width : 2 * width] + parts[:, 2 * width :]


def stencil_term(own, position, edge_codes):
    bin_count = lax.axis_size("bin")
    row_count, width = own.shape
    group_size = row_count // bin_count
    grid_rows, grid_cols = edge_codes.shape
    payload = jnp.concatenate([own, position.astype(jnp.float32)[:, None]], 1)
    got = lax.all_to_all(
        payload.reshape(bin_count, group_size * (width + 1)), "bin", 0, 0, tiled=True
    ).reshape(row_count, width + 1)
    tile_slot = got[:, width].astype(jnp.int32) - lax.axis_index("bin") * row_count
    cells = lax.broadcasted_iota(jnp.int32, (row_count, row_count), 1)
    onehot = (tile_slot[:, None] == cells).astype(jnp.bfloat16)
    placed = lax.dot_general(
        onehot,
        split_three(got[:, :width]),
        (((0,), (0,)), ((), ())),
        preferred_element_type=jnp.float32,
    )
    tile_rows = join_three(placed, width)
    cell_scale = edge_codes.astype(jnp.float32) / 8.0
    weighted = cell_scale[:, :, None] * tile_rows.reshape(grid_rows, grid_cols, width)
    rim_last, rim_first = (weighted[-1], weighted[0])
    upper_rows, upper_scale = passed_along((rim_last, cell_scale[-1]), "bin", 1)
    lower_rows, lower_scale = passed_along((rim_first, cell_scale[0]), "bin", -1)
    degree_grid = (
        cell_scale * neighbour_first(cell_scale[None], upper_scale[None], lower_scale[None])[0]
    )
    smooth_grid = cell_scale[:, :, None] * neighbour_sum(weighted, upper_rows, lower_rows)
    back = jnp.concatenate(
        [smooth_grid.reshape(row_count, width), degree_grid.reshape(row_count, 1)], 1
    )
    back_rows = join_three(
        jnp.dot(onehot, split_three(back), preferred_element_type=jnp.float32), width + 1
    )
    ret = lax.all_to_all(
        back_rows.reshape(bin_count, group_size * (width + 1)), "bin", 0, 0, tiled=True
    ).reshape(row_count, width + 1)
    return (ret[:, :width], ret[:, width])


def on_device(counts, factors, loadings, position, edge_codes):
    bin_count = lax.axis_size("bin")
    gene_count = lax.axis_size("gene")
    row_count, width_all = factors.shape
    group_size = row_count // bin_count
    width = width_all // gene_count
    k_rows = width_all // bin_count
    gene_at = lax.axis_index("gene")
    bin_at = lax.axis_index("bin")
    load_bf = loadings.astype(jnp.bfloat16)
    right_dims = (((1,), (1,)), ((), ()))
    numer_part = lax.dot_general(counts, load_bf, right_dims, preferred_element_type=jnp.float32)
    gram_part = lax.dot_general(load_bf, load_bf, right_dims, preferred_element_type=jnp.float32)
    both = lax.psum_scatter(
        jnp.concatenate([numer_part, gram_part], 0), "gene", scatter_dimension=1, tiled=True
    )
    numer, load_gram = (both[:row_count], both[row_count:])
    own = lax.dynamic_slice_in_dim(factors, gene_at * width, width, 1)
    smooth, degree = stencil_term(own, position, edge_codes)
    penalty = float(G * K) / 64.0
    denom = (
        jnp.dot(factors, load_gram, precision=lax.Precision.HIGHEST)
        + penalty * degree[:, None] * own
    )
    new_own = own * (numer + penalty * smooth) / denom
    factors_new = lax.all_gather(new_own, "gene", axis=1, tiled=True)
    fac_bf = factors_new.astype(jnp.bfloat16)
    left_dims = (((0,), (0,)), ((), ()))
    cross_part = lax.dot_general(fac_bf, counts, left_dims, preferred_element_type=jnp.float32)
    fgram_part = lax.dot_general(fac_bf, fac_bf, left_dims, preferred_element_type=jnp.float32)
    both_bin = lax.psum_scatter(
        jnp.concatenate([cross_part, fgram_part], 1), "bin", scatter_dimension=0, tiled=True
    )
    cross, fac_gram = (both_bin[:, : cross_part.shape[1]], both_bin[:, cross_part.shape[1] :])
    own_load = lax.dynamic_slice_in_dim(loadings, bin_at * k_rows, k_rows, 0)
    new_load = own_load * cross / jnp.dot(fac_gram, loadings, precision=lax.Precision.HIGHEST)
    loadings_new = lax.all_gather(new_load, "bin", axis=0, tiled=True)
    return (factors_new, loadings_new)


def solution(mesh):
    placed = (P("bin", "gene"), P("bin", None), P(None, "gene"), P("bin"), P("bin", None))
    return jax.shard_map(
        on_device,
        mesh=mesh,
        in_specs=placed,
        out_specs=(P("bin", None), P(None, "gene")),
        check_vma=False,
    )
```

profile of v0, /device:TPU:1, one launch (start us, length us, event | category | flops | bytes accessed | tf_op | source)
XLA Modules:
  0.0 368.8 jit_solution(11523954443179676951)
XLA Ops:
  16.0 3.8 %all_to_all.16 = f32[16,1,6336]{2,1,0:T(1,128)} reshape(f32[3072,33]{1,0:T(8,128)} %copy.30) | data formatting | bytes 811008 | tf_op jit(solution)/shard_map/all_to_all | solution.py:52
  19.9 9.3 %all-to-all-start = ((f32[16,1,6336]{2,1,0:T(1,128)}), f32[16,1,6336]{2,1,0:T(1,128)}, u32[]{:S(2)}, u32[]{:S(2)}) async-start(f32[16,1,6336]{2,1,0:T(1,128)} %all_to_all.16), calls=%async_computation | async-start | bytes 819200 | tf_op jit(solution)/shard_map/all_to_all | solution.py:52
  32.7 5.0 %collective-permute-start.3 = (f32[256]{0:T(256)}, f32[256]{0:T(256)}, u32[]{:S(2)}, u32[]{:S(2)}) collective-permute-start(f32[256]{0:T(256)} %bitcast.6), channel_id=1, source_target_pairs={{0,1},{1,2},{2,3},{3,4},{4,5},{5,6},{6,7},{7,8},{8,9},{9,10},{10,1... | collective-permute-start | bytes 3080 | tf_op jit(solution)/shard_map/ppermute | solution.py:13
  37.8 2.9 fusion.23
  40.7 7.2 %fusion.25 = f32[3072,256]{1,0:T(8,128)S(1)} fusion(bf16[3072,2304]{1,0:T(8,128)(2,1)} %param.5, f32[256,2304]{1,0:T(8,128)S(1)} %copy-done.2), kind=kOutput, calls=%fused_computation.36 | convolution fusion | flops 3624468480 | bytes 19660800 | tf_op jit(solution)/shard_map/dot_general | solution.py:97
  49.9 5.0 %copy.41 = f32[3328,256]{0,1:T(8,128)} copy(f32[3328,256]{1,0:T(8,128)} %pad_maximum_fusion) | data formatting | bytes 6815744
  58.2 2.7 reduce
  61.0 4.0 %reshape.94 = f32[3072,33]{1,0:T(8,128)} reshape(f32[16,6336]{1,0:T(8,128)} %reduce) | data formatting | bytes 811008 | tf_op jit(solution)/shard_map/reshape | solution.py:54
  64.9 2.9 copy.44
  71.2 7.5 %fusion.1 = f32[3072,96]{0,1:T(8,128)S(1)} fusion(s32[3072]{0:T(1024)S(1)} %fusion.8, bf16[3072,32]{0,1:T(8,128)(2,1)S(1)} %get-tuple-element.16, bf16[3072,32]{0,1:T(8,128)(2,1)S(1)} %get-tuple-element.17, bf16[3072,32]{0,1:T(8,128)(2,1)S(1)} %get-tuple-element.15), kind=kOutput, calls=%fused_computation.2 | convolution fusion | flops 1823145984 | bytes 1781760 | tf_op jit(solution)/shard_map/dot_general | solution.py:58
  84.6 5.3 %collective-permute-start.1 = (f32[256,32]{0,1:T(8,128)S(1)}, f32[256,32]{0,1:T(8,128)S(1)}, u32[]{:S(2)}, u32[]{:S(2)}) collective-permute-start(f32[256,32]{0,1:T(8,128)S(1)} %bitcast.56), channel_id=1, source_target_pairs={{0,1},{1,2},{2,3},{3,4},{4,5},{5,6},{6,7},{7,8},{8,9},{9,10},{10,1... | collective-permute-start | bytes 98312 | tf_op jit(solution)/shard_map/ppermute | solution.py:13
  95.5 8.0 %fusion = f32[3072,99]{0,1:T(8,128)S(1)} fusion(s32[3072]{0:T(1024)S(1)} %copy-done.6, bf16[3072,33]{0,1:T(8,128)(2,1)S(1)} %get-tuple-element.13, bf16[3072,33]{0,1:T(8,128)(2,1)S(1)} %get-tuple-element.14, bf16[3072,33]{0,1:T(8,128)(2,1)S(1)} %get-tuple-element.12), kind=kOutput, calls=%fused_computation.1 | convolution fusion | flops 1879824384 | bytes 1837056 | tf_op jit(solution)/shard_map/dot_general | solution.py:78
  107.1 3.8 %all_to_all.17 = f32[16,1,6336]{2,1,0:T(1,128)} reshape(f32[3072,33]{1,0:T(8,128)} %copy.35) | data formatting | bytes 811008 | tf_op jit(solution)/shard_map/all_to_all | solution.py:80
  111.0 25.5 %all_to_all.20 = f32[16,1,6336]{2,1,0:T(1,128)} all-to-all(f32[16,1,6336]{2,1,0:T(1,128)} %all_to_all.17), channel_id=1, replica_groups=mesh['gene'=8,'bin'=16] {'bin'}, dimensions={0} | all-to-all | bytes 811008 | tf_op jit(solution)/shard_map/all_to_all | solution.py:80
  136.4 2.7 reduce.2
  139.2 4.0 %reshape.98 = f32[3072,33]{1,0:T(8,128)} reshape(f32[16,6336]{1,0:T(8,128)} %reduce.2) | data formatting | bytes 811008 | tf_op jit(solution)/shard_map/reshape | solution.py:82
  148.1 4.8 %fusion.5 = f32[3072,32]{0,1:T(8,128)} fusion(f32[3072,256]{1,0:T(8,128)S(1)} %copy-done, f32[3072,32]{0,1:T(8,128)S(1)} %copy.43, f32[3328,32]{0,1:T(8,128)} %bitcast.57, f32[3072,32]{0,1:T(8,128)} %copy.47, f32[3072]{0:T(1024)S(1)} %fusion.6), kind=kOutput, calls=%fused_computation.7 | convolution fusion | flops 302579712 | bytes 4763648 | tf_op jit(solution)/shard_map/dot_general | solution.py:107
  153.0 68.1 %all-gather.3.cloned.1.call-done = f32[3072,256]{0,1:T(8,128)} async-done(((f32[3072,32]{0,1:T(8,128)}), f32[3072,256]{0,1:T(8,128)}) %all-gather.3.cloned.1.call-update) | async-done | bytes 3145744 | tf_op jit(solution)/shard_map/all_gather | solution.py:111
  221.1 10.3 %fusion.11 = f32[256,2304]{1,0:T(8,128)S(1)} fusion(bf16[3072,2304]{1,0:T(8,128)(2,1)} %param.5, f32[3072,256]{0,1:T(8,128)} %all-gather.3.cloned.1.call-done), kind=kOutput, calls=%fused_computation.18 | convolution fusion | flops 3624665088 | bytes 19660800 | tf_op jit(solution)/shard_map/dot_general | solution.py:114
  234.0 71.9 %reduce-scatter.5.cloned.1.call-done = f32[16,2560]{1,0:T(8,128)} async-done(((f32[256,2560]{1,0:T(8,128)}), f32[16,2560]{1,0:T(8,128)}) %reduce-scatter.5.cloned.1.call-update) | async-done | bytes 163856 | tf_op jit(solution)/shard_map/reduce_scatter | solution.py:116
  305.9 3.5 convolution_divide_fusion
  309.5 3.5 copy.39
  313.0 45.8 %all-gather.5.cloned.1.call-done = f32[256,2304]{1,0:T(8,128)} async-done(((f32[16,2304]{1,0:T(8,128)}), f32[256,2304]{1,0:T(8,128)}) %all-gather.5.cloned.1.call-update) | async-done | bytes 2359312 | tf_op jit(solution)/shard_map/all_gather | solution.py:122
  358.8 3.2 copy.57
  (67 shorter events, 43.5 us)
Async XLA Ops:
  7.2 1.9 copy-start
  9.1 3.5 copy-start.7
  19.9 38.4 %all-to-all-start = ((f32[16,1,6336]{2,1,0:T(1,128)}), f32[16,1,6336]{2,1,0:T(1,128)}, u32[]{:S(2)}, u32[]{:S(2)}) async-start(f32[16,1,6336]{2,1,0:T(1,128)} %all_to_all.16), calls=%async_computation | async-start | bytes 819200 | tf_op jit(solution)/shard_map/all_to_all | solution.py:52
  29.2 118.9 %reduce-scatter.7.cloned.1.call-start = ((), (), s32[]{:S(2)}) async-start(), calls=%async_computation.7 | async-start | bytes 3833856
  29.2 11.5 %copy-start.2 = (f32[256,2304]{1,0:T(8,128)S(1)}, f32[256,2304]{1,0:T(8,128)}, u32[]{:S(2)}) copy-start(f32[256,2304]{1,0:T(8,128)} %param.7) | copy-start | bytes 7077892
  30.1 7.7 %copy-start.3 = (f32[12,256]{1,0:T(8,128)}, f32[12,256]{1,0:T(8,128)S(1)}, u32[]{:S(2)}) copy-start(f32[12,256]{1,0:T(8,128)S(1)} %get-tuple-element.25) | copy-start | bytes 36868
  30.7 26.1 %collective-permute-start.2 = (f32[256]{0:T(256)}, f32[256]{0:T(256)}, u32[]{:S(2)}, u32[]{:S(2)}) collective-permute-start(f32[256]{0:T(256)} %bitcast.4), channel_id=1, source_target_pairs={{1,0},{2,1},{3,2},{4,3},{5,4},{6,5},{7,6},{8,7},{9,8},{10,9},{11,1... | collective-permute-start | bytes 3080 | tf_op jit(solution)/shard_map/ppermute | solution.py:13
  32.7 24.0 %collective-permute-start.3 = (f32[256]{0:T(256)}, f32[256]{0:T(256)}, u32[]{:S(2)}, u32[]{:S(2)}) collective-permute-start(f32[256]{0:T(256)} %bitcast.6), channel_id=1, source_target_pairs={{0,1},{1,2},{2,3},{3,4},{4,5},{5,6},{6,7},{7,8},{8,9},{9,10},{10,1... | collective-permute-start | bytes 3080 | tf_op jit(solution)/shard_map/ppermute | solution.py:13
  55.0 166.1 %all-gather.3.cloned.1.call-start = ((), (), s32[]{:S(2)}) async-start(), calls=%async_computation.4 | async-start | bytes 3538944 | tf_op jit(solution)/shard_map/all_gather | solution.py:111
  70.1 8.6 %copy-start.5 = (s32[3072]{0:T(1024)}, s32[3072]{0:T(1024)S(1)}, u32[]{:S(2)}) copy-start(s32[3072]{0:T(1024)S(1)} %fusion.8) | copy-start | bytes 36868
  78.8 2.7 copy-start.4
  82.6 7.6 %collective-permute-start = (f32[256,32]{0,1:T(8,128)S(1)}, f32[256,32]{0,1:T(8,128)S(1)}, u32[]{:S(2)}, u32[]{:S(2)}) collective-permute-start(f32[256,32]{0,1:T(8,128)S(1)} %bitcast.55), channel_id=1, source_target_pairs={{1,0},{2,1},{3,2},{4,3},{5,4},{6,5},{7,6},{8,7},{9,8},{10,9},{11,1... | collective-permute-start | bytes 98312 | tf_op jit(solution)/shard_map/ppermute | solution.py:13
  84.6 6.9 %collective-permute-start.1 = (f32[256,32]{0,1:T(8,128)S(1)}, f32[256,32]{0,1:T(8,128)S(1)}, u32[]{:S(2)}, u32[]{:S(2)}) collective-permute-start(f32[256,32]{0,1:T(8,128)S(1)} %bitcast.56), channel_id=1, source_target_pairs={{0,1},{1,2},{2,3},{3,4},{4,5},{5,6},{6,7},{7,8},{8,9},{9,10},{10,1... | collective-permute-start | bytes 98312 | tf_op jit(solution)/shard_map/ppermute | solution.py:13
  91.8 3.8 %copy-start.6 = (s32[3072]{0:T(1024)S(1)}, s32[3072]{0:T(1024)}, u32[]{:S(2)}) copy-start(s32[3072]{0:T(1024)} %copy-done.5) | copy-start | bytes 36868
  152.9 153.0 %reduce-scatter.5.cloned.1.call-start = ((), (), s32[]{:S(2)}) async-start(), calls=%async_computation.5 | async-start | bytes 2785280 | tf_op jit(solution)/shard_map/reduce_scatter | solution.py:116
  221.1 10.3 %copy-start.1 = (f32[3072,256]{0,1:T(8,128)S(1)}, f32[3072,256]{0,1:T(8,128)}, u32[]{:S(2)}) copy-start(f32[3072,256]{0,1:T(8,128)} %all-gather.3.cloned.1.call-done) | copy-start | bytes 9437188
  233.9 124.9 %all-gather.5.cloned.1.call-start = ((), (), s32[]{:S(2)}) async-start(), calls=%async_computation.6 | async-start | bytes 2506752 | tf_op jit(solution)/shard_map/all_gather | solution.py:122
Sparse Core Ops, SparseCore 0:
  55.1 83.0 reduce-scatter.6
  153.0 68.0 all-gather.2
  234.0 71.8 reduce-scatter.4
  309.6 49.1 all-gather.4
where the time goes:
time: 375 us; the launch traced here: 369 us
  waiting for transfers between devices  187 us (50%)
  local copies, waits for them, and re-layouts  50.9 us (14%)
  matrix products  45 us (12%)
  blocking collectives  25.5 us (7%)
  starting transfers between devices  24.2 us (6%)
  other arithmetic  21.8 us (6%)
  between operations  14.3 us (4%)
    reduce_scatter x1, waiting for transfers between devices, on_device(): lax.psum_scatter(jnp.concatenate([cross_part, fgram_part], 1), 'bin', sca...  71.9 us
    all_gather x1, waiting for transfers between devices, on_device(): factors_new = lax.all_gather(new_own, 'gene', axis=1, tiled=True)  68.1 us
    all_gather x1, waiting for transfers between devices, on_device(): loadings_new = lax.all_gather(new_load, 'bin', axis=0, tiled=True)  45.8 us
    all_to_all x1, blocking collectives, stencil_term(): lax.all_to_all(back_rows.reshape(bin_count, group_size * (width + 1)), 'b...  25.5 us
    unnamed x27, local copies, waits for them, and re-layouts  22.6 us
    ppermute x4, starting transfers between devices, passed_along(): return lax.ppermute(block, axis, route)  14.3 us
    dot_general x1, matrix products, on_device(): lax.dot_general(fac_bf, counts, left_dims, preferred_element_type=jnp.flo...  10.3 us
    all_to_all x1, starting transfers between devices, stencil_term(): lax.all_to_all(payload.reshape(bin_count, group_size * (width + 1)), 'bin...  9.29 us
  transfers between devices with their start and end apart: 9, of which 4 were waited for; matrix products, arithmetic and copies ran while one was open for 21% of the time, Pallas kernels for 0%

commit v1 on v0

--- a/solution.py
+++ b/solution.py
@@ -84,6 +84,12 @@
 
 
 def on_device(counts, factors, loadings, position, edge_codes):
+
+    def press_bars_in(u, across):
+        return jnp.concatenate(
+            lax.all_to_all(jnp.stack(lax.axis_size(across) * [u], 0), across, 0, 0), 1
+        )
+
     bin_count = lax.axis_size("bin")
     gene_count = lax.axis_size("gene")
     row_count, width_all = factors.shape
@@ -108,7 +114,7 @@
         + penalty * degree[:, None] * own
     )
     new_own = own * (numer + penalty * smooth) / denom
-    factors_new = lax.all_gather(new_own, "gene", axis=1, tiled=True)
+    factors_new = press_bars_in(new_own, "gene")
     fac_bf = factors_new.astype(jnp.bfloat16)
     left_dims = (((0,), (0,)), ((), ()))
     cross_part = lax.dot_general(fac_bf, counts, left_dims, preferred_element_type=jnp.float32)

time: 375 us -> 343 us (0.915)
  waiting for transfers between devices: 187 us -> 116 us
  blocking collectives: 25.5 us -> 67.1 us
    all_gather x1 -> x0, waiting for transfers between devices: 68.1 us -> none  [on_device(): factors_new = lax.all_gather(new_own, 'gene', axis=1, tiled=True)]
    all_to_all x0 -> x1, blocking collectives: none -> 41.6 us  [press_bars_in(): lax.all_to_all(jnp.stack(lax.axis_size(across) * [u], 0), across, 0, 0)]
  transfers between devices with their start and end apart: 9 -> 8, of which waited for: 4 -> 3; matrix products, arithmetic and copies ran while one was open for 21% -> 23% of each run, Pallas kernels for 0% -> 0%
where the time goes in v1:
time: 343 us; the launch traced here: 337 us
  waiting for transfers between devices  116 us (34%)
  blocking collectives  67.1 us (20%)
  local copies, waits for them, and re-layouts  51.3 us (15%)
  matrix products  42.6 us (12%)
  starting transfers between devices  24.2 us (7%)
  other arithmetic  22 us (6%)
  between operations  14.3 us (4%)
    reduce_scatter x1, waiting for transfers between devices, on_device(): lax.psum_scatter(jnp.concatenate([cross_part, fgram_part], 1), 'bin', sca...  68.7 us
    all_gather x1, waiting for transfers between devices, on_device(): loadings_new = lax.all_gather(new_load, 'bin', axis=0, tiled=True)  45.8 us
    all_to_all x1, blocking collectives, press_bars_in(): lax.all_to_all(jnp.stack(lax.axis_size(across) * [u], 0), across, 0, 0)  41.6 us
    all_to_all x1, blocking collectives, stencil_term(): lax.all_to_all(back_rows.reshape(bin_count, group_size * (width + 1)), 'b...  25.5 us
    unnamed x27, local copies, waits for them, and re-layouts  22.6 us
    ppermute x4, starting transfers between devices, passed_along(): return lax.ppermute(block, axis, route)  14.3 us
    all_to_all x1, starting transfers between devices, stencil_term(): lax.all_to_all(payload.reshape(bin_count, group_size * (width + 1)), 'bin...  9.29 us
    dot_general x1, matrix products, on_device(): lax.dot_general(fac_bf, counts, left_dims, preferred_element_type=jnp.flo...  8.71 us
  transfers between devices with their start and end apart: 8, of which 3 were waited for; matrix products, arithmetic and copies ran while one was open for 23% of the time, Pallas kernels for 0%

profile of v1, /device:TPU:1, one launch (start us, length us, event | category | flops | bytes accessed | tf_op | source)
XLA Modules:
  0.0 337.2 jit_solution(11375970078732196236)
XLA Ops:
  16.0 3.8 %all_to_all.20 = f32[16,1,6336]{2,1,0:T(1,128)} reshape(f32[3072,33]{1,0:T(8,128)} %copy.32) | data formatting | bytes 811008 | tf_op jit(solution)/shard_map/all_to_all | solution.py:52
  19.9 9.3 %all-to-all-start = ((f32[16,1,6336]{2,1,0:T(1,128)}), f32[16,1,6336]{2,1,0:T(1,128)}, u32[]{:S(2)}, u32[]{:S(2)}) async-start(f32[16,1,6336]{2,1,0:T(1,128)} %all_to_all.20), calls=%async_computation | async-start | bytes 819200 | tf_op jit(solution)/shard_map/all_to_all | solution.py:52
  32.7 5.0 %collective-permute-start.3 = (f32[256]{0:T(256)}, f32[256]{0:T(256)}, u32[]{:S(2)}, u32[]{:S(2)}) collective-permute-start(f32[256]{0:T(256)} %bitcast.6), channel_id=1, source_target_pairs={{0,1},{1,2},{2,3},{3,4},{4,5},{5,6},{6,7},{7,8},{8,9},{9,10},{10,1... | collective-permute-start | bytes 3080 | tf_op jit(solution)/shard_map/ppermute | solution.py:13
  37.8 2.9 fusion.21
  40.7 7.2 %fusion.23 = f32[3072,256]{1,0:T(8,128)S(1)} fusion(bf16[3072,2304]{1,0:T(8,128)(2,1)} %param.5, f32[256,2304]{1,0:T(8,128)S(1)} %copy-done.2), kind=kOutput, calls=%fused_computation.35 | convolution fusion | flops 3624468480 | bytes 19660800 | tf_op jit(solution)/shard_map/dot_general | solution.py:103
  49.9 5.0 %copy.43 = f32[3328,256]{0,1:T(8,128)} copy(f32[3328,256]{1,0:T(8,128)} %pad_maximum_fusion) | data formatting | bytes 6815744
  58.3 2.7 reduce
  61.0 4.0 %reshape.104 = f32[3072,33]{1,0:T(8,128)} reshape(f32[16,6336]{1,0:T(8,128)} %reduce) | data formatting | bytes 811008 | tf_op jit(solution)/shard_map/reshape | solution.py:54
  65.0 2.9 copy.46
  71.2 7.5 %fusion.1 = f32[3072,96]{0,1:T(8,128)S(1)} fusion(s32[3072]{0:T(1024)S(1)} %fusion.8, bf16[3072,32]{0,1:T(8,128)(2,1)S(1)} %get-tuple-element.18, bf16[3072,32]{0,1:T(8,128)(2,1)S(1)} %get-tuple-element.19, bf16[3072,32]{0,1:T(8,128)(2,1)S(1)} %get-tuple-element.17), kind=kOutput, calls=%fused_computation.2 | convolution fusion | flops 1823145984 | bytes 1781760 | tf_op jit(solution)/shard_map/dot_general | solution.py:58
  84.6 5.3 %collective-permute-start.1 = (f32[256,32]{0,1:T(8,128)S(1)}, f32[256,32]{0,1:T(8,128)S(1)}, u32[]{:S(2)}, u32[]{:S(2)}) collective-permute-start(f32[256,32]{0,1:T(8,128)S(1)} %bitcast.66), channel_id=1, source_target_pairs={{0,1},{1,2},{2,3},{3,4},{4,5},{5,6},{6,7},{7,8},{8,9},{9,10},{10,1... | collective-permute-start | bytes 98312 | tf_op jit(solution)/shard_map/ppermute | solution.py:13
  95.5 8.0 %fusion = f32[3072,99]{0,1:T(8,128)S(1)} fusion(s32[3072]{0:T(1024)S(1)} %copy-done.6, bf16[3072,33]{0,1:T(8,128)(2,1)S(1)} %get-tuple-element.15, bf16[3072,33]{0,1:T(8,128)(2,1)S(1)} %get-tuple-element.16, bf16[3072,33]{0,1:T(8,128)(2,1)S(1)} %get-tuple-element.14), kind=kOutput, calls=%fused_computation.1 | convolution fusion | flops 1879824384 | bytes 1837056 | tf_op jit(solution)/shard_map/dot_general | solution.py:78
  107.1 3.8 %all_to_all.21 = f32[16,1,6336]{2,1,0:T(1,128)} reshape(f32[3072,33]{1,0:T(8,128)} %copy.37) | data formatting | bytes 811008 | tf_op jit(solution)/shard_map/all_to_all | solution.py:80
  111.0 25.5 %all_to_all.25 = f32[16,1,6336]{2,1,0:T(1,128)} all-to-all(f32[16,1,6336]{2,1,0:T(1,128)} %all_to_all.21), channel_id=1, replica_groups=mesh['gene'=8,'bin'=16] {'bin'}, dimensions={0} | all-to-all | bytes 811008 | tf_op jit(solution)/shard_map/all_to_all | solution.py:80
  136.5 2.7 reduce.2
  139.2 4.0 %reshape.108 = f32[3072,33]{1,0:T(8,128)} reshape(f32[16,6336]{1,0:T(8,128)} %reduce.2) | data formatting | bytes 811008 | tf_op jit(solution)/shard_map/reshape | solution.py:82
  148.1 4.1 %fusion.5 = f32[3072,32]{0,1:T(8,128)S(1)} fusion(f32[3072,256]{1,0:T(8,128)S(1)} %copy-done, f32[3072,32]{0,1:T(8,128)S(1)} %copy.45, f32[3328,32]{0,1:T(8,128)} %bitcast.67, f32[3072,32]{0,1:T(8,128)} %copy.49, f32[3072]{0:T(1024)S(1)} %fusion.6), kind=kOutput, calls=%fused_computation.7 | convolution fusion | flops 302579712 | bytes 4763648 | tf_op jit(solution)/shard_map/dot_general | solution.py:113
  152.5 41.6 %all_to_all.26 = f32[8,3072,32]{1,2,0:T(8,128)S(1)} all-to-all(f32[8,3072,32]{1,2,0:T(8,128)S(1)} %stack.2), channel_id=1, replica_groups=mesh['gene'=8,'bin'=16] {'gene'}, dimensions={0} | all-to-all | bytes 6291456 | tf_op jit(solution)/shard_map/all_to_all | solution.py:90
  194.1 8.7 %fusion.9 = f32[256,2304]{1,0:T(8,128)S(1)} fusion(bf16[3072,2304]{1,0:T(8,128)(2,1)} %param.5, f32[3072,256]{0,1:T(8,128)S(1)} %bitcast.55), kind=kOutput, calls=%fused_computation.17 | convolution fusion | flops 3624665088 | bytes 19660800 | tf_op jit(solution)/shard_map/dot_general | solution.py:120
  205.6 68.7 %reduce-scatter.5.cloned.1.call-done = f32[16,2560]{1,0:T(8,128)} async-done(((f32[256,2560]{1,0:T(8,128)}), f32[16,2560]{1,0:T(8,128)}) %reduce-scatter.5.cloned.1.call-update) | async-done | bytes 163856 | tf_op jit(solution)/shard_map/reduce_scatter | solution.py:122
  274.3 3.5 %convolution_divide_fusion = f32[16,2304]{1,0:T(8,128)} fusion(f32[256,2304]{1,0:T(8,128)} %param.7, f32[16,2560]{1,0:T(8,128)} %reduce-scatter.5.cloned.1.call-done, s32[]{:T(128)S(6)} %select_n.7), kind=kOutput, calls=%fused_computation.9 | convolution fusion | flops 113319936 | bytes 2818052 | tf_op jit(solution)/shard_map/dot_general | solution.py:127
  277.9 3.5 %copy.41 = f32[3072,256]{1,0:T(8,128)} copy(f32[3072,256]{0,1:T(8,128)} %bitcast.56) | data formatting | bytes 6291456
  281.4 45.8 %all-gather.2.cloned.1.call-done = f32[256,2304]{1,0:T(8,128)} async-done(((f32[16,2304]{1,0:T(8,128)}), f32[256,2304]{1,0:T(8,128)}) %all-gather.2.cloned.1.call-update) | async-done | bytes 2359312 | tf_op jit(solution)/shard_map/all_gather | solution.py:128
  327.2 3.2 copy.59
  (67 shorter events, 44.0 us)
Async XLA Ops:
  7.2 1.9 copy-start
  9.1 3.5 %copy-start.7 = (s32[3072]{0:T(1024)S(1)}, s32[3072]{0:T(1024)}, u32[]{:S(2)}) copy-start(s32[3072]{0:T(1024)} %param.8) | copy-start | bytes 36868
  19.9 38.4 %all-to-all-start = ((f32[16,1,6336]{2,1,0:T(1,128)}), f32[16,1,6336]{2,1,0:T(1,128)}, u32[]{:S(2)}, u32[]{:S(2)}) async-start(f32[16,1,6336]{2,1,0:T(1,128)} %all_to_all.20), calls=%async_computation | async-start | bytes 819200 | tf_op jit(solution)/shard_map/all_to_all | solution.py:52
  29.2 118.9 %reduce-scatter.7.cloned.1.call-start = ((), (), s32[]{:S(2)}) async-start(), calls=%async_computation.7 | async-start | bytes 3833856
  29.2 11.5 %copy-start.2 = (f32[256,2304]{1,0:T(8,128)S(1)}, f32[256,2304]{1,0:T(8,128)}, u32[]{:S(2)}) copy-start(f32[256,2304]{1,0:T(8,128)} %param.7) | copy-start | bytes 7077892
  30.1 7.7 %copy-start.3 = (f32[12,256]{1,0:T(8,128)}, f32[12,256]{1,0:T(8,128)S(1)}, u32[]{:S(2)}) copy-start(f32[12,256]{1,0:T(8,128)S(1)} %get-tuple-element.27) | copy-start | bytes 36868
  30.7 26.1 %collective-permute-start.2 = (f32[256]{0:T(256)}, f32[256]{0:T(256)}, u32[]{:S(2)}, u32[]{:S(2)}) collective-permute-start(f32[256]{0:T(256)} %bitcast.4), channel_id=1, source_target_pairs={{1,0},{2,1},{3,2},{4,3},{5,4},{6,5},{7,6},{8,7},{9,8},{10,9},{11,1... | collective-permute-start | bytes 3080 | tf_op jit(solution)/shard_map/ppermute | solution.py:13
  32.7 24.0 %collective-permute-start.3 = (f32[256]{0:T(256)}, f32[256]{0:T(256)}, u32[]{:S(2)}, u32[]{:S(2)}) collective-permute-start(f32[256]{0:T(256)} %bitcast.6), channel_id=1, source_target_pairs={{0,1},{1,2},{2,3},{3,4},{4,5},{5,6},{6,7},{7,8},{8,9},{9,10},{10,1... | collective-permute-start | bytes 3080 | tf_op jit(solution)/shard_map/ppermute | solution.py:13
  55.0 219.3 %reduce-scatter.5.cloned.1.call-start = ((), (), s32[]{:S(2)}) async-start(), calls=%async_computation.5 | async-start | bytes 2785280 | tf_op jit(solution)/shard_map/reduce_scatter | solution.py:122
  70.1 8.6 %copy-start.5 = (s32[3072]{0:T(1024)}, s32[3072]{0:T(1024)S(1)}, u32[]{:S(2)}) copy-start(s32[3072]{0:T(1024)S(1)} %fusion.8) | copy-start | bytes 36868
  78.8 2.7 copy-start.4
  82.6 7.6 %collective-permute-start = (f32[256,32]{0,1:T(8,128)S(1)}, f32[256,32]{0,1:T(8,128)S(1)}, u32[]{:S(2)}, u32[]{:S(2)}) collective-permute-start(f32[256,32]{0,1:T(8,128)S(1)} %bitcast.65), channel_id=1, source_target_pairs={{1,0},{2,1},{3,2},{4,3},{5,4},{6,5},{7,6},{8,7},{9,8},{10,9},{11,1... | collective-permute-start | bytes 98312 | tf_op jit(solution)/shard_map/ppermute | solution.py:13
  84.6 6.9 %collective-permute-start.1 = (f32[256,32]{0,1:T(8,128)S(1)}, f32[256,32]{0,1:T(8,128)S(1)}, u32[]{:S(2)}, u32[]{:S(2)}) collective-permute-start(f32[256,32]{0,1:T(8,128)S(1)} %bitcast.66), channel_id=1, source_target_pairs={{0,1},{1,2},{2,3},{3,4},{4,5},{5,6},{6,7},{7,8},{8,9},{9,10},{10,1... | collective-permute-start | bytes 98312 | tf_op jit(solution)/shard_map/ppermute | solution.py:13
  91.8 3.8 %copy-start.6 = (s32[3072]{0:T(1024)S(1)}, s32[3072]{0:T(1024)}, u32[]{:S(2)}) copy-start(s32[3072]{0:T(1024)} %copy-done.5) | copy-start | bytes 36868
  194.1 8.7 %copy-start.1 = (f32[8,3072,32]{1,2,0:T(8,128)}, f32[8,3072,32]{1,2,0:T(8,128)S(1)}, u32[]{:S(2)}) copy-start(f32[8,3072,32]{1,2,0:T(8,128)S(1)} %all_to_all.26) | copy-start | bytes 9437188
  205.6 121.7 %all-gather.2.cloned.1.call-start = ((), (), s32[]{:S(2)}) async-start(), calls=%async_computation.6 | async-start | bytes 2506752 | tf_op jit(solution)/shard_map/all_gather | solution.py:128
Sparse Core Ops, SparseCore 0:
  55.1 83.0 reduce-scatter.6
  205.7 68.5 reduce-scatter.4
  278.0 49.2 all-gather.1
